TPU v7x, 32 devices: a whole 2x2x4 slice. The times are simulated.
32 devices in a mesh: prow: 4 (over y, x), pcol: 8 (over z, core).
Axes of the slice: x: 2, y: 2, z: 4, core: 2. Of those that a mesh axis runs over, the one named last changes fastest.
Arguments:
- anc_inverse: bfloat16 [6, 1024, 3, 2048], P(None, 'prow', None, 'pcol'), may hold values from -0.078125 to 0.078125
- panel: bfloat16 [3, 6, 4, 256, 512], P(None, None, 'prow', 'pcol'), may hold values from -1.1953125 to 1.1953125
- tile_mask: int32 [3, 24], replicated, may hold values 0 or 1
- diag_inverse: float32 [3, 512, 512], P(None, ('prow', 'pcol')), may hold values from -6 to 6
Outputs:
- block_column: bfloat16 [3, 6, 4, 256, 512], P(None, None, 'prow', 'pcol')
- diag_block: float32 [3, 512, 512], P(None, ('prow', 'pcol'))
All inputs are finite; a program needn't handle non-finite values.
Results may differ from a plain program's by a relative error of at most 0.0017.
Values may be sent and summed in bfloat16 or wider, within the bound.
No kernel may reach another device: no remote copies, remote signals or barrier semaphores. Data moves between devices by JAX's collectives and lax.ppermute only.
A program may use at most 128 MiB of HBM per device.

v0:
```python
import jax
import jax.numpy as jnp
from jax import lax
from jax.sharding import PartitionSpec as P


def spread(x, axis, root):
    mine = lax.axis_index(axis) == root
    return lax.psum(jnp.where(mine, x, jnp.zeros_like(x)), axis)


def local_product(anc_block, columns):
    return jnp.einsum("aibj,sbjw->isaw", anc_block, columns, preferred_element_type=jnp.float32)


def outbound(masked, n_row, n_col):
    groups, tile_rows, single, sub_rows, width = masked.shape
    tile_cols = tile_rows * n_row // n_col
    grouped = masked.reshape(groups, tile_cols, n_col // n_row, sub_rows, width)
    return jnp.repeat(grouped, n_row, axis=2)


def body(anc_inverse, panel, tile_mask, diag_inverse):
    n_row = lax.axis_size("prow")
    n_col = lax.axis_size("pcol")
    row_pos = lax.axis_index("prow")
    col_pos = lax.axis_index("pcol")
    sets, tile_rows, single, sub_rows, width = panel.shape
    tiles = tile_mask.shape[1]
    tile_size = anc_inverse.shape[1]
    row_ids = jnp.arange(tile_rows, dtype=jnp.int32) * n_row + row_pos
    hits = (row_ids[:, None] == jnp.arange(tiles, dtype=jnp.int32)[None, :]).astype(jnp.int32)
    row_mask = jnp.sum(tile_mask[:, None, :] * hits[None], axis=2)
    keep = row_mask.astype(jnp.bfloat16)[:, :, None, None, None]
    masked = panel * keep
    outgoing = outbound(masked, n_row, n_col)
    root = col_pos % n_row
    arrived = lax.all_to_all(outgoing, "pcol", split_axis=2, concat_axis=3, tiled=True)
    columns = spread(arrived.reshape(sets, -1, tile_size, width), "prow", root)
    summed = lax.psum_scatter(
        local_product(anc_inverse, columns), "pcol", scatter_dimension=0, tiled=True
    )
    image = -jnp.transpose(summed, (1, 2, 0, 3))[:, :, None] * keep.astype(jnp.float32)
    block_column = image.astype(jnp.bfloat16)
    partial_value = jnp.einsum(
        "saxiw,saxiv->swv", masked, block_column, preferred_element_type=jnp.float32
    )
    mine = lax.psum_scatter(partial_value, ("prow", "pcol"), scatter_dimension=1, tiled=True)
    diag_block = diag_inverse - mine
    return (block_column, diag_block)


def solution(mesh):
    in_specs = (
        P(None, "prow", None, "pcol"),
        P(None, None, "prow", "pcol", None),
        P(),
        P(None, ("prow", "pcol"), None),
    )
    out_specs = (P(None, None, "prow", "pcol", None), P(None, ("prow", "pcol"), None))
    return jax.shard_map(body, mesh=mesh, in_specs=in_specs, out_specs=out_specs, check_vma=False)
```

profile of v0, /device:TPU:0, one launch (start us, length us, event | category | flops | bytes accessed | tf_op | source)
XLA Modules:
  0.0 455.2 jit_solution(3141937686562053441)
XLA Ops:
  7.2 0.0 copy-start
  7.2 0.1 fusion.6
  7.3 1.0 multiply_reduce_fusion
  8.2 1.2 broadcast_multiply_fusion
  9.4 0.0 copy-start.1
  9.4 0.8 copy-done.1
  10.3 1.7 broadcast_in_dim.4
  12.0 6.4 %all-to-all-start = ((bf16[3,3,8,32,512]{4,3,1,0,2:T(8,128)(2,1)}), bf16[3,3,8,32,512]{4,3,1,0,2:T(8,128)(2,1)}, u32[]{:S(2)}, u32[]{:S(2)}) async-start(bf16[3,3,8,32,512]{4,3,1,0,2:T(8,128)(2,1)} %bitcast.27), calls=%async_computation | async-start | bytes 4718592 | tf_op jit(solution)/shard_map/all_to_all | solution.py:38
  18.4 0.0 all-reduce.2.cloned.1.call-start
  18.4 54.7 %all-to-all-done = bf16[3,3,8,32,512]{4,3,1,0,2:T(8,128)(2,1)} async-done(((bf16[3,3,8,32,512]{4,3,1,0,2:T(8,128)(2,1)}), bf16[3,3,8,32,512]{4,3,1,0,2:T(8,128)(2,1)}, u32[]{:S(2)}, u32[]{:S(2)}) %all-to-all-start) | async-done | bytes 2359328 | tf_op jit(solution)/shard_map/all_to_all | solution.py:38
  73.1 3.2 copy_select_fusion
  76.3 4.3 copy.20
  80.6 0.0 all-reduce.2.cloned.1.call-update
  80.6 0.0 reduce-scatter.3.cloned.1.call-start
  80.7 72.9 %all-reduce.2.cloned.1.call-done = bf16[3,3,256,512]{2,3,1,0:T(8,128)(2,1)} async-done(((bf16[3,3,256,512]{2,3,1,0:T(8,128)(2,1)}), bf16[3,3,256,512]{2,3,1,0:T(8,128)(2,1)}) %all-reduce.2.cloned.1.call-update) | async-done | bytes 2359312 | tf_op jit(solution)/shard_map/psum | solution.py:9
  153.6 0.0 copy-done
  153.6 7.9 %convolution_bitcast_fusion = f32[256,3,6,512]{0,3,2,1:T(8,128)} fusion(bf16[3,3,256,512]{2,3,1,0:T(8,128)(2,1)} %all-reduce.2.cloned.1.call-done, bf16[6,256,3,256]{3,1,2,0:T(8,128)(2,1)S(1)} %copy-done), kind=kOutput, calls=%fused_computation | convolution fusion | flops 3623878656 | bytes 14155776 | tf_op jit(solution)/shard_map/aibj,sbjw->isaw/dot_general | solution.py:13
  161.5 11.9 %copy.21 = f32[256,3,6,512]{3,2,1,0:T(8,128)} copy(f32[256,3,6,512]{0,3,2,1:T(8,128)} %convolution_bitcast_fusion) | data formatting | bytes 18874368 | tf_op jit(solution)/shard_map/aibj,sbjw->isaw/transpose | solution.py:13
  173.4 0.0 reduce-scatter.3.cloned.1.call-update
  173.4 0.0 reduce-scatter.5.cloned.1.call-start
  173.4 129.2 %reduce-scatter.3.cloned.1.call-done = f32[32,3,6,512]{3,2,1,0:T(8,128)} async-done(((f32[256,3,6,512]{3,2,1,0:T(8,128)}), f32[32,3,6,512]{3,2,1,0:T(8,128)}) %reduce-scatter.3.cloned.1.call-update) | async-done | bytes 1179664 | tf_op jit(solution)/shard_map/reduce_scatter | solution.py:40
  302.7 1.8 fusion.5
  304.4 3.4 convolution_bitcast_fusion.1
  307.8 0.0 copy-start.2
  307.8 0.0 reduce-scatter.5.cloned.1.call-update
  307.8 1.0 copy.23
  308.8 138.3 %reduce-scatter.5.cloned.1.call-done = f32[3,16,512]{2,1,0:T(8,128)} async-done(((f32[3,512,512]{2,1,0:T(8,128)}), f32[3,16,512]{2,1,0:T(8,128)}) %reduce-scatter.5.cloned.1.call-update) | async-done | bytes 98320 | tf_op jit(solution)/shard_map/reduce_scatter | solution.py:48
  447.1 0.0 copy-done.2
  447.1 1.5 sub.3
  (3 shorter events, 0.1 us)
Async XLA Ops:
  7.2 146.4 %copy-start = (bf16[6,256,3,256]{3,1,2,0:T(8,128)(2,1)S(1)}, bf16[6,256,3,256]{3,1,2,0:T(8,128)(2,1)}, u32[]{:S(2)}) copy-start(bf16[6,256,3,256]{3,1,2,0:T(8,128)(2,1)} %param.4) | copy-start | bytes 7077892
  9.4 0.8 copy-start.1
  12.0 61.1 %all-to-all-start = ((bf16[3,3,8,32,512]{4,3,1,0,2:T(8,128)(2,1)}), bf16[3,3,8,32,512]{4,3,1,0,2:T(8,128)(2,1)}, u32[]{:S(2)}, u32[]{:S(2)}) async-start(bf16[3,3,8,32,512]{4,3,1,0,2:T(8,128)(2,1)} %bitcast.27), calls=%async_computation | async-start | bytes 4718592 | tf_op jit(solution)/shard_map/all_to_all | solution.py:38
  18.4 135.2 %all-reduce.2.cloned.1.call-start = ((), (), s32[]{:S(2)}) async-start(), calls=%async_computation.3 | async-start | bytes 4718592 | tf_op jit(solution)/shard_map/psum | solution.py:9
  80.6 222.0 %reduce-scatter.3.cloned.1.call-start = ((), (), s32[]{:S(2)}) async-start(), calls=%async_computation.4 | async-start | bytes 14155776 | tf_op jit(solution)/shard_map/reduce_scatter | solution.py:40
  173.4 273.7 %reduce-scatter.5.cloned.1.call-start = ((), (), s32[]{:S(2)}) async-start(), calls=%async_computation.5 | async-start | bytes 3244032 | tf_op jit(solution)/shard_map/reduce_scatter | solution.py:48
  307.8 139.3 %copy-start.2 = (f32[3,16,512]{2,1,0:T(8,128)S(1)}, f32[3,16,512]{2,1,0:T(8,128)}, u32[]{:S(2)}) copy-start(f32[3,16,512]{2,1,0:T(8,128)} %param.7) | copy-start | bytes 294916
Sparse Core Ops, SparseCore 0:
  80.7 72.7 all-reduce.1
  173.5 129.1 reduce-scatter.2
  308.0 139.0 reduce-scatter.4
where the time goes:
time: 456 us; the launch traced here: 455 us
  waiting for transfers between devices  395 us (87%)
  local copies, waits for them, and re-layouts  19.7 us (4%)
  between operations  13.8 us (3%)
  matrix products  11.3 us (2%)
  other arithmetic  8.76 us (2%)
  starting transfers between devices  6.47 us (1%)
    reduce_scatter x1, waiting for transfers between devices, body(): lax.psum_scatter(partial_value, ('prow', 'pcol'), scatter_dimension=1, ti...  138 us
    reduce_scatter x1, waiting for transfers between devices, body(): lax.psum_scatter(local_product(anc_inverse, columns), 'pcol', scatter_dim...  129 us
    psum x1, waiting for transfers between devices, spread(): return lax.psum(jnp.where(mine, x, jnp.zeros_like(x)), axis)  72.9 us
    all_to_all x1, waiting for transfers between devices, body(): lax.all_to_all(outgoing, 'pcol', split_axis=2, concat_axis=3, tiled=True)  54.7 us
    transpose x1, local copies, waits for them, and re-layouts, local_product(): jnp.einsum('aibj,sbjw->isaw', anc_block, columns, preferred_element_type=...  11.9 us
  transfers between devices with their start and end apart: 4, of which 4 were waited for; matrix products, arithmetic and copies ran while one was open for 0% of the time, Pallas kernels for 0%

commit v1 on v0

--- a/solution.py
+++ b/solution.py
@@ -35,7 +35,15 @@
     masked = panel * keep
     outgoing = outbound(masked, n_row, n_col)
     root = col_pos % n_row
-    arrived = lax.all_to_all(outgoing, "pcol", split_axis=2, concat_axis=3, tiled=True)
+    ways, here = (lax.axis_size("pcol"), lax.axis_index("pcol"))
+    width_2 = outgoing.shape[2] // ways
+    turned = jnp.roll(outgoing, -here * width_2, axis=2)
+    got = [lax.slice_in_dim(turned, 0, width_2, axis=2)]
+    for far in range(1, ways):
+        sent = lax.slice_in_dim(turned, far * width_2, (far + 1) * width_2, axis=2)
+        got.append(lax.ppermute(sent, "pcol", [(d, (d + far) % ways) for d in range(ways)]))
+    line = jnp.concatenate(got[::-1], axis=3)
+    arrived = jnp.roll(line, (here + 1) * got[0].shape[3], axis=3)
     columns = spread(arrived.reshape(sets, -1, tile_size, width), "prow", root)
     summed = lax.psum_scatter(
         local_product(anc_inverse, columns), "pcol", scatter_dimension=0, tiled=True

time: 456 us -> 478 us (1.048)
  local copies, waits for them, and re-layouts: 19.7 us -> 53.7 us
  waiting for transfers between devices: 395 us -> 369 us
  starting transfers between devices: 6.47 us -> 15.9 us
    all_to_all x1 -> x0, waiting for transfers between devices: 54.7 us -> none  [body(): lax.all_to_all(outgoing, 'pcol', split_axis=2, concat_axis=3, tiled=True)]
    ppermute x0 -> x7, waiting for transfers between devices: none -> 26.2 us  [body(): lax.ppermute(sent, 'pcol', [(d, (d + far) % ways) for d in range(ways)])]
    concatenate x0 -> x1, local copies, waits for them, and re-layouts: none -> 19.8 us  [body(): arrived = jnp.roll(line, (here + 1) * got[0].shape[3], axis=3)]
    ppermute x0 -> x7, local copies, waits for them, and re-layouts: none -> 16.8 us  [body(): lax.ppermute(sent, 'pcol', [(d, (d + far) % ways) for d in range(ways)])]
    ppermute x0 -> x7, starting transfers between devices: none -> 15.8 us  [body(): lax.ppermute(sent, 'pcol', [(d, (d + far) % ways) for d in range(ways)])]
    all_to_all x1 -> x0, starting transfers between devices: 6.35 us -> none  [body(): lax.all_to_all(outgoing, 'pcol', split_axis=2, concat_axis=3, tiled=True)]
  transfers between devices with their start and end apart: 4 -> 10, of which waited for: 4 -> 6; matrix products, arithmetic and copies ran while one was open for 0% -> 4% of each run, Pallas kernels for 0% -> 0%
where the time goes in v1:
time: 478 us; the launch traced here: 475 us
  waiting for transfers between devices  369 us (77%)
  local copies, waits for them, and re-layouts  53.7 us (11%)
  starting transfers between devices  15.9 us (3%)
  between operations  13.9 us (3%)
  other arithmetic  11.3 us (2%)
  matrix products  11.3 us (2%)
    reduce_scatter x1, waiting for transfers between devices, body(): lax.psum_scatter(partial_value, ('prow', 'pcol'), scatter_dimension=1, ti...  138 us
    reduce_scatter x1, waiting for transfers between devices, body(): lax.psum_scatter(local_product(anc_inverse, columns), 'pcol', scatter_dim...  129 us
    psum x1, waiting for transfers between devices, spread(): return lax.psum(jnp.where(mine, x, jnp.zeros_like(x)), axis)  75.5 us
    ppermute x7, waiting for transfers between devices, body(): lax.ppermute(sent, 'pcol', [(d, (d + far) % ways) for d in range(ways)])  26.2 us
    concatenate x1, local copies, waits for them, and re-layouts, body(): arrived = jnp.roll(line, (here + 1) * got[0].shape[3], axis=3)  19.8 us
    ppermute x7, local copies, waits for them, and re-layouts, body(): lax.ppermute(sent, 'pcol', [(d, (d + far) % ways) for d in range(ways)])  16.8 us
    ppermute x7, starting transfers between devices, body(): lax.ppermute(sent, 'pcol', [(d, (d + far) % ways) for d in range(ways)])  15.8 us
    transpose x1, local copies, waits for them, and re-layouts, local_product(): jnp.einsum('aibj,sbjw->isaw', anc_block, columns, preferred_element_type=...  11.9 us
  transfers between devices with their start and end apart: 10, of which 6 were waited for; matrix products, arithmetic and copies ran while one was open for 4% of the time, Pallas kernels for 0%

profile of v1, /device:TPU:0, one launch (start us, length us, event | category | flops | bytes accessed | tf_op | source)
XLA Modules:
  0.0 475.2 jit_solution(18076619949485335907)
XLA Ops:
  7.2 0.0 copy-start
  7.2 0.0 all-reduce.2.cloned.1.call-start
  7.3 0.1 fusion.7
  7.3 1.0 multiply_reduce_fusion
  8.3 1.2 broadcast_multiply_fusion
  9.5 0.0 copy-start.1
  9.5 0.3 broadcast_in_dim.4
  9.8 0.5 copy-done.1
  10.3 0.8 fusion
  11.2 1.3 fusion.9
  12.4 4.5 collective-permute-start
  16.9 0.0 collective-permute-start.6
  16.9 0.1 collective-permute-start.3
  17.0 1.3 collective-permute-start.1
  18.4 3.6 collective-permute-start.2
  22.0 2.4 collective-permute-done
  24.4 0.0 copy-start.2
  24.4 6.3 %collective-permute-start.4 = (bf16[3,3,1,32,512]{4,3,2,1,0:T(8,128)(2,1)}, bf16[3,3,1,32,512]{4,3,2,1,0:T(8,128)(2,1)}, u32[]{:S(2)}, u32[]{:S(2)}) collective-permute-start(bf16[3,3,1,32,512]{4,3,2,1,0:T(8,128)(2,1)} %get-tuple-element.12), channel_id=1, source_target_pairs={{0,3},{1,4},{2,5},{3,6},{4,7},{5,0},{6,1},{7,2},{8,11},{9,12},{10,... | collective-permute-start | bytes 884744 | tf_op jit(solution)/shard_map/ppermute | solution.py:44
  30.7 0.0 collective-permute-done.6
  30.7 0.0 copy-done.2
  30.7 0.0 copy-start.3
  30.7 0.7 copy-done.3
  31.4 0.0 collective-permute-start.5
  31.4 1.5 copy.70
  32.9 2.4 copy.48
  35.3 2.4 copy.42
  37.7 0.0 collective-permute-done.1
  37.7 2.4 copy.43
  40.1 3.4 collective-permute-done.2
  43.5 2.4 copy.44
  45.9 0.0 collective-permute-done.3
  45.9 2.4 copy.45
  48.3 20.4 %collective-permute-done.4 = bf16[3,3,1,32,512]{4,3,2,1,0:T(8,128)(2,1)} collective-permute-done((bf16[3,3,1,32,512]{4,3,2,1,0:T(8,128)(2,1)}, bf16[3,3,1,32,512]{4,3,2,1,0:T(8,128)(2,1)}, u32[]{:S(2)}, u32[]{:S(2)}) %collective-permute-start.4) | collective-permute-done | bytes 294944 | tf_op jit(solution)/shard_map/ppermute | solution.py:44
  68.7 2.4 copy.46
  71.1 0.0 collective-permute-done.5
  71.1 2.4 copy.47
  73.5 19.8 %concatenate.11 = bf16[3,3,1,512,512]{3,4,1,0,2:T(8,128)(2,1)} concatenate(bf16[3,3,1,32,512]{3,4,1,0,2:T(8,128)(2,1)} %copy.42, bf16[3,3,1,32,512]{3,4,1,0,2:T(8,128)(2,1)} %copy.43, bf16[3,3,1,32,512]{3,4,1,0,2:T(8,128)(2,1)} %copy.44, bf16[3,3,1,32,512]{3,4,1,0,2:T(8,128)(2,1)} %copy.45, bf16[3,3,1,32,512]{3,4,1,0,2:T(8,128)(2,1)} %copy.46, bf16[3,3,1,32,512]{3,4,1,0,2:T(8,128)(2,1)} %copy.47, ...), dimensions={3} | concatenate | bytes 9437184 | tf_op jit(solution)/shard_map/jit(_roll_dynamic)/concatenate | solution.py:46
  93.3 4.9 %select_bitcast_fusion = bf16[3,3,256,512]{2,3,1,0:T(8,128)(2,1)} fusion(bf16[3,3,1,512,512]{3,4,1,0,2:T(8,128)(2,1)} %concatenate.11, s32[]{:T(128)S(6)} %select_n.45, pred[]{:T(512)S(6)} %eq.27), kind=kLoop, calls=%fused_computation.6 | loop fusion | flops 1179648 | bytes 4718597 | tf_op jit(solution)/shard_map/jit(_where)/select_n | solution.py:9
  98.2 0.0 all-reduce.2.cloned.1.call-update
  98.2 0.0 reduce-scatter.3.cloned.1.call-start
  98.3 75.5 %all-reduce.2.cloned.1.call-done = bf16[3,3,256,512]{2,3,1,0:T(8,128)(2,1)} async-done(((bf16[3,3,256,512]{2,3,1,0:T(8,128)(2,1)}), bf16[3,3,256,512]{2,3,1,0:T(8,128)(2,1)}) %all-reduce.2.cloned.1.call-update) | async-done | bytes 2359312 | tf_op jit(solution)/shard_map/psum | solution.py:9
  173.7 0.0 copy-done
  173.7 7.9 %convolution_bitcast_fusion = f32[256,3,6,512]{0,3,2,1:T(8,128)} fusion(bf16[3,3,256,512]{2,3,1,0:T(8,128)(2,1)} %all-reduce.2.cloned.1.call-done, bf16[6,256,3,256]{3,1,2,0:T(8,128)(2,1)S(1)} %copy-done), kind=kOutput, calls=%fused_computation.2 | convolution fusion | flops 3623878656 | bytes 14155776 | tf_op jit(solution)/shard_map/aibj,sbjw->isaw/dot_general | solution.py:13
  181.7 11.9 %copy.56 = f32[256,3,6,512]{3,2,1,0:T(8,128)} copy(f32[256,3,6,512]{0,3,2,1:T(8,128)} %convolution_bitcast_fusion) | data formatting | bytes 18874368 | tf_op jit(solution)/shard_map/aibj,sbjw->isaw/transpose | solution.py:13
  193.6 0.0 reduce-scatter.3.cloned.1.call-update
  193.6 0.0 reduce-scatter.5.cloned.1.call-start
  193.6 129.2 %reduce-scatter.3.cloned.1.call-done = f32[32,3,6,512]{3,2,1,0:T(8,128)} async-done(((f32[256,3,6,512]{3,2,1,0:T(8,128)}), f32[32,3,6,512]{3,2,1,0:T(8,128)}) %reduce-scatter.3.cloned.1.call-update) | async-done | bytes 1179664 | tf_op jit(solution)/shard_map/reduce_scatter | solution.py:48
  322.9 1.8 fusion.6
  324.6 3.4 convolution_bitcast_fusion.1
  328.0 0.0 copy-start.4
  328.0 0.0 reduce-scatter.5.cloned.1.call-update
  328.0 1.0 copy.58
  329.0 138.2 %reduce-scatter.5.cloned.1.call-done = f32[3,16,512]{2,1,0:T(8,128)} async-done(((f32[3,512,512]{2,1,0:T(8,128)}), f32[3,16,512]{2,1,0:T(8,128)}) %reduce-scatter.5.cloned.1.call-update) | async-done | bytes 98320 | tf_op jit(solution)/shard_map/reduce_scatter | solution.py:56
  467.2 0.0 copy-done.4
  467.2 1.5 sub.13
  (2 shorter events, 0.0 us)
Async XLA Ops:
  7.2 166.6 %copy-start = (bf16[6,256,3,256]{3,1,2,0:T(8,128)(2,1)S(1)}, bf16[6,256,3,256]{3,1,2,0:T(8,128)(2,1)}, u32[]{:S(2)}) copy-start(bf16[6,256,3,256]{3,1,2,0:T(8,128)(2,1)} %param.4) | copy-start | bytes 7077892
  7.2 166.5 %all-reduce.2.cloned.1.call-start = ((), (), s32[]{:S(2)}) async-start(), calls=%async_computation.2 | async-start | bytes 4718592 | tf_op jit(solution)/shard_map/psum | solution.py:9
  9.5 0.8 copy-start.1
  12.4 12.0 %collective-permute-start = (bf16[3,3,1,32,512]{4,3,2,1,0:T(8,128)(2,1)S(1)}, bf16[3,3,1,32,512]{4,3,2,1,0:T(8,128)(2,1)S(1)}, u32[]{:S(2)}, u32[]{:S(2)}) collective-permute-start(bf16[3,3,1,32,512]{4,3,2,1,0:T(8,128)(2,1)S(1)} %get-tuple-element.16), channel_id=1, source_target_pairs={{0,7},{1,0},{2,1},{3,2},{4,3},{5,4},{6,5},{7,6},{8,15},{9,8},{10,9... | collective-permute-start | bytes 884744 | tf_op jit(solution)/shard_map/ppermute | solution.py:44
  16.9 13.7 %collective-permute-start.6 = (bf16[3,3,1,32,512]{4,3,2,1,0:T(8,128)(2,1)S(1)}, bf16[3,3,1,32,512]{4,3,2,1,0:T(8,128)(2,1)S(1)}, u32[]{:S(2)}, u32[]{:S(2)}) collective-permute-start(bf16[3,3,1,32,512]{4,3,2,1,0:T(8,128)(2,1)S(1)} %get-tuple-element.17), channel_id=1, source_target_pairs={{0,1},{1,2},{2,3},{3,4},{4,5},{5,6},{6,7},{7,0},{8,9},{9,10},{10,1... | collective-permute-start | bytes 884744 | tf_op jit(solution)/shard_map/ppermute | solution.py:44
  16.9 29.0 %collective-permute-start.3 = (bf16[3,3,1,32,512]{4,3,2,1,0:T(8,128)(2,1)}, bf16[3,3,1,32,512]{4,3,2,1,0:T(8,128)(2,1)}, u32[]{:S(2)}, u32[]{:S(2)}) collective-permute-start(bf16[3,3,1,32,512]{4,3,2,1,0:T(8,128)(2,1)} %get-tuple-element.13), channel_id=1, source_target_pairs={{0,4},{1,5},{2,6},{3,7},{4,0},{5,1},{6,2},{7,3},{8,12},{9,13},{10,... | collective-permute-start | bytes 884744 | tf_op jit(solution)/shard_map/ppermute | solution.py:44
  17.0 20.7 %collective-permute-start.1 = (bf16[3,3,1,32,512]{4,3,2,1,0:T(8,128)(2,1)}, bf16[3,3,1,32,512]{4,3,2,1,0:T(8,128)(2,1)}, u32[]{:S(2)}, u32[]{:S(2)}) collective-permute-start(bf16[3,3,1,32,512]{4,3,2,1,0:T(8,128)(2,1)} %get-tuple-element.15), channel_id=1, source_target_pairs={{0,6},{1,7},{2,0},{3,1},{4,2},{5,3},{6,4},{7,5},{8,14},{9,15},{10,... | collective-permute-start | bytes 884744 | tf_op jit(solution)/shard_map/ppermute | solution.py:44
  18.4 25.1 %collective-permute-start.2 = (bf16[3,3,1,32,512]{4,3,2,1,0:T(8,128)(2,1)}, bf16[3,3,1,32,512]{4,3,2,1,0:T(8,128)(2,1)}, u32[]{:S(2)}, u32[]{:S(2)}) collective-permute-start(bf16[3,3,1,32,512]{4,3,2,1,0:T(8,128)(2,1)} %get-tuple-element.14), channel_id=1, source_target_pairs={{0,5},{1,6},{2,7},{3,0},{4,1},{5,2},{6,3},{7,4},{8,13},{9,14},{10,... | collective-permute-start | bytes 884744 | tf_op jit(solution)/shard_map/ppermute | solution.py:44
  24.4 6.3 %copy-start.2 = (bf16[3,3,1,32,512]{4,3,2,1,0:T(8,128)(2,1)}, bf16[3,3,1,32,512]{4,3,2,1,0:T(8,128)(2,1)S(1)}, u32[]{:S(2)}) copy-start(bf16[3,3,1,32,512]{4,3,2,1,0:T(8,128)(2,1)S(1)} %collective-permute-done) | copy-start | bytes 884740
  24.4 44.3 %collective-permute-start.4 = (bf16[3,3,1,32,512]{4,3,2,1,0:T(8,128)(2,1)}, bf16[3,3,1,32,512]{4,3,2,1,0:T(8,128)(2,1)}, u32[]{:S(2)}, u32[]{:S(2)}) collective-permute-start(bf16[3,3,1,32,512]{4,3,2,1,0:T(8,128)(2,1)} %get-tuple-element.12), channel_id=1, source_target_pairs={{0,3},{1,4},{2,5},{3,6},{4,7},{5,0},{6,1},{7,2},{8,11},{9,12},{10,... | collective-permute-start | bytes 884744 | tf_op jit(solution)/shard_map/ppermute | solution.py:44
  30.7 0.7 copy-start.3
  31.4 39.6 %collective-permute-start.5 = (bf16[3,3,1,32,512]{4,3,2,1,0:T(8,128)(2,1)}, bf16[3,3,1,32,512]{4,3,2,1,0:T(8,128)(2,1)}, u32[]{:S(2)}, u32[]{:S(2)}) collective-permute-start(bf16[3,3,1,32,512]{4,3,2,1,0:T(8,128)(2,1)} %get-tuple-element.11), channel_id=1, source_target_pairs={{0,2},{1,3},{2,4},{3,5},{4,6},{5,7},{6,0},{7,1},{8,10},{9,11},{10,... | collective-permute-start | bytes 884744 | tf_op jit(solution)/shard_map/ppermute | solution.py:44
  98.2 224.6 %reduce-scatter.3.cloned.1.call-start = ((), (), s32[]{:S(2)}) async-start(), calls=%async_computation.3 | async-start | bytes 14155776 | tf_op jit(solution)/shard_map/reduce_scatter | solution.py:48
  193.6 273.6 %reduce-scatter.5.cloned.1.call-start = ((), (), s32[]{:S(2)}) async-start(), calls=%async_computation.4 | async-start | bytes 3244032 | tf_op jit(solution)/shard_map/reduce_scatter | solution.py:56
  328.0 139.2 %copy-start.4 = (f32[3,16,512]{2,1,0:T(8,128)S(1)}, f32[3,16,512]{2,1,0:T(8,128)}, u32[]{:S(2)}) copy-start(f32[3,16,512]{2,1,0:T(8,128)} %param.7) | copy-start | bytes 294916
Sparse Core Ops, SparseCore 0:
  98.3 75.3 all-reduce.1
  193.7 129.1 reduce-scatter.2
  328.1 138.9 reduce-scatter.4
